TPU v7x, 256 devices: a whole 4x4x8 slice. The times are simulated.
256 devices in a mesh: tm: 32 (over y, x, core), head: 8 (over z).
Axes of the slice: x: 4, y: 4, z: 8, core: 2. Of those that a mesh axis runs over, the one named last changes fastest.
Arguments:
- query_act: bfloat16 [8192, 3072], P('tm', 'head'), may hold values from -160 to 160
- key_act: bfloat16 [8192, 3072], P('tm', 'head'), may hold values from -7 to 7
- value_act: bfloat16 [8192, 3072], P('tm', 'head'), may hold values from -6 to 6
- d_output: bfloat16 [8192, 3072], P('tm', 'head'), may hold values from -6 to 6
- out_weight: bfloat16 [3072, 3072], P('head'), may hold values from -0.15625 to 0.15625
- block_mask: int32 [64, 64], P('tm'), may hold values from 0 to 1, as said below
Outputs:
- output: bfloat16 [8192, 3072], P('tm', 'head')
- d_query: bfloat16 [8192, 3072], P('tm', 'head')
- d_key: bfloat16 [8192, 3072], P('tm', 'head')
- d_value: bfloat16 [8192, 3072], P('tm', 'head')
Inputs may be any that keep to these rules, and one draw needn't show every extreme that they name: With g(b) = b // 2 the frame group of block b: block_mask[a, b] is 1 whenever g(a) == g(b), and 0 unless |g(a) - g(b)| is 0, 1, 2, 3 or 4.
All inputs are finite; a program needn't handle non-finite values.
Results may differ from a plain program's by a relative error of at most 0.033.
Values may be sent and summed in bfloat16 or wider, within the bound.
No kernel may reach another device: no remote copies, remote signals or barrier semaphores. Data moves between devices by JAX's collectives and lax.ppermute only.
A program may use at most 64 MiB of HBM per device.

v0:
```python
import jax
import jax.numpy as jnp
from jax import lax
from jax.sharding import PartitionSpec as P

HEAD_DIM = 128
BLOCK = 128


def from_behind(value, axis, steps):
    count = lax.axis_size(axis)
    initial, last = (max(0, -steps), min(count, count - steps))
    return lax.ppermute(value, axis, [(source, source + steps) for source in range(initial, last)])


def local(query_act, key_act, value_act, d_output, out_weight, block_mask):
    row_count = query_act.shape[0]
    col_count = query_act.shape[1]
    score_scale = HEAD_DIM ** (-0.5)
    tm_count = lax.axis_size("tm")
    tm_index = lax.axis_index("tm")
    per_group = row_count // BLOCK
    kv_pair = jnp.stack([key_act, value_act])
    shards = {0: kv_pair}
    upward = kv_pair
    downward = kv_pair
    for relay_step in range(4):
        upward = from_behind(upward, "tm", 1)
        downward = from_behind(downward, "tm", -1)
        shards[relay_step + 1] = upward
        shards[-(relay_step + 1)] = downward
    offsets = (0, 1, 2, 3, 4, -1, -2, -3, -4)
    keys_all = jnp.concatenate([shards[offset][0] for offset in offsets], 0)
    values_all = jnp.concatenate([shards[offset][1] for offset in offsets], 0)
    mask_blocks = []
    for offset in offsets:
        source = tm_index - offset
        inside = (source >= 0) & (source < tm_count)
        start_col = jnp.clip(source, 0, tm_count - 1) * per_group
        mask_cols = lax.dynamic_slice_in_dim(block_mask, start_col, per_group, 1)
        mask_blocks.append((mask_cols == 1) & inside)
    allowed = jnp.repeat(jnp.repeat(jnp.concatenate(mask_blocks, 1), BLOCK, 0), BLOCK, 1)
    heads_here = col_count // HEAD_DIM
    prob_list = []
    attn_list = []
    for head_pos in range(heads_here):
        lower = head_pos * HEAD_DIM
        q_head = query_act[:, lower : lower + HEAD_DIM]
        k_head = keys_all[:, lower : lower + HEAD_DIM]
        v_head = values_all[:, lower : lower + HEAD_DIM]
        scores = (
            lax.dot_general(
                q_head, k_head, (((1,), (1,)), ((), ())), preferred_element_type=jnp.float32
            )
            * score_scale
        )
        masked = jnp.where(allowed, scores, -jnp.inf)
        top = jnp.max(masked, axis=1, keepdims=True)
        expo = jnp.exp(masked - top)
        probs = expo / jnp.sum(expo, axis=1, keepdims=True)
        weights = probs.astype(jnp.bfloat16)
        prob_list.append(probs)
        attn_list.append(
            jnp.dot(weights, v_head, preferred_element_type=jnp.float32).astype(jnp.bfloat16)
        )
    attn = jnp.concatenate(attn_list, 1)
    projected = jnp.dot(attn, out_weight, preferred_element_type=jnp.float32)
    output = lax.psum_scatter(
        projected.astype(jnp.bfloat16), "head", scatter_dimension=1, tiled=True
    )
    d_attn = lax.dot_general(
        lax.all_gather(d_output, "head", axis=1, tiled=True),
        out_weight,
        (((1,), (1,)), ((), ())),
        preferred_element_type=jnp.float32,
    ).astype(jnp.bfloat16)
    dq_list = []
    dk_list = []
    dv_list = []
    for head_pos in range(heads_here):
        lower = head_pos * HEAD_DIM
        q_head = query_act[:, lower : lower + HEAD_DIM]
        k_head = keys_all[:, lower : lower + HEAD_DIM]
        v_head = values_all[:, lower : lower + HEAD_DIM]
        grad_head = d_attn[:, lower : lower + HEAD_DIM]
        attn_head = attn[:, lower : lower + HEAD_DIM]
        probs = prob_list[head_pos]
        weights = probs.astype(jnp.bfloat16)
        delta = jnp.sum(
            grad_head.astype(jnp.float32) * attn_head.astype(jnp.float32), axis=1, keepdims=True
        )
        d_probs = lax.dot_general(
            grad_head, v_head, (((1,), (1,)), ((), ())), preferred_element_type=jnp.float32
        )
        d_scores = (score_scale * probs * (d_probs - delta)).astype(jnp.bfloat16)
        dq_list.append(
            jnp.dot(d_scores, k_head, preferred_element_type=jnp.float32).astype(jnp.bfloat16)
        )
        dk_list.append(
            lax.dot_general(
                d_scores, q_head, (((0,), (0,)), ((), ())), preferred_element_type=jnp.float32
            )
        )
        dv_list.append(
            lax.dot_general(
                weights, grad_head, (((0,), (0,)), ((), ())), preferred_element_type=jnp.float32
            )
        )
    d_query = jnp.concatenate(dq_list, 1)
    dk_all = jnp.concatenate(dk_list, 1)
    dv_all = jnp.concatenate(dv_list, 1)
    partials = {}
    for position, offset in enumerate(offsets):
        lower_row = position * row_count
        partials[offset] = jnp.stack(
            [dk_all[lower_row : lower_row + row_count], dv_all[lower_row : lower_row + row_count]]
        )
    grad_sum = partials[0]
    carried_up = jnp.zeros_like(grad_sum)
    carried_down = jnp.zeros_like(grad_sum)
    for distance in (4, 3, 2, 1):
        carried_up = carried_up + partials[distance]
        carried_down = carried_down + partials[-distance]
        carried_up = from_behind(carried_up.astype(jnp.bfloat16), "tm", -1).astype(carried_up.dtype)
        carried_down = from_behind(carried_down.astype(jnp.bfloat16), "tm", 1).astype(
            carried_down.dtype
        )
    grad_sum = grad_sum + carried_up + carried_down
    d_key = grad_sum[0].astype(jnp.bfloat16)
    d_value = grad_sum[1].astype(jnp.bfloat16)
    return (output, d_query, d_key, d_value)


def solution(mesh):
    placed = (
        P("tm", "head"),
        P("tm", "head"),
        P("tm", "head"),
        P("tm", "head"),
        P("head", None),
        P("tm", None),
    )
    return jax.shard_map(
        local,
        mesh=mesh,
        in_specs=placed,
        out_specs=(P("tm", "head"), P("tm", "head"), P("tm", "head"), P("tm", "head")),
        check_vma=False,
    )
```

profile of v0, /device:TPU:7, one launch (start us, length us, event | category | flops | bytes accessed | tf_op | source)
XLA Modules:
  0.0 157.3 jit_solution(2815863973381337522)
XLA Ops:
  7.2 2.0 %pad_maximum_fusion.2 = bf16[2,256,384]{2,1,0:T(8,128)(2,1)} fusion(bf16[1,256,384]{2,1,0:T(8,128)(2,1)} %bitcast.147, bf16[1,256,384]{2,1,0:T(8,128)(2,1)} %bitcast.146), kind=kLoop, calls=%fused_computation.81 | loop fusion | flops 196608 | bytes 786432 | tf_op jit(solution)/shard_map/stack | solution.py:23
  9.2 3.7 %collective-permute-start = (bf16[2,256,384]{2,1,0:T(8,128)(2,1)}, bf16[2,256,384]{2,1,0:T(8,128)(2,1)S(1)}, u32[]{:S(2)}, u32[]{:S(2)}) collective-permute-start(bf16[2,256,384]{2,1,0:T(8,128)(2,1)} %pad_maximum_fusion.2), channel_id=1, source_target_pairs={{0,8},{8,16},{16,24},{24,32},{32,40},{40,48},{48,56},{56,64},{64,7... | collective-permute-start | bytes 1179656 | tf_op jit(solution)/shard_map/ppermute | solution.py:13
  12.9 1.9 %collective-permute-start.4 = (bf16[2,256,384]{2,1,0:T(8,128)(2,1)}, bf16[2,256,384]{2,1,0:T(8,128)(2,1)S(1)}, u32[]{:S(2)}, u32[]{:S(2)}) collective-permute-start(bf16[2,256,384]{2,1,0:T(8,128)(2,1)} %pad_maximum_fusion.2), channel_id=1, source_target_pairs={{8,0},{16,8},{24,16},{32,24},{40,32},{48,40},{56,48},{64,56},{72,6... | collective-permute-start | bytes 1179656 | tf_op jit(solution)/shard_map/ppermute | solution.py:13
  14.8 3.1 %collective-permute-done = bf16[2,256,384]{2,1,0:T(8,128)(2,1)S(1)} collective-permute-done((bf16[2,256,384]{2,1,0:T(8,128)(2,1)}, bf16[2,256,384]{2,1,0:T(8,128)(2,1)S(1)}, u32[]{:S(2)}, u32[]{:S(2)}) %collective-permute-start) | collective-permute-done | bytes 393248 | tf_op jit(solution)/shard_map/ppermute | solution.py:13
  17.9 6.4 %collective-permute-start.1 = (bf16[2,256,384]{2,1,0:T(8,128)(2,1)S(1)}, bf16[2,256,384]{2,1,0:T(8,128)(2,1)S(1)}, u32[]{:S(2)}, u32[]{:S(2)}) collective-permute-start(bf16[2,256,384]{2,1,0:T(8,128)(2,1)S(1)} %collective-permute-done), channel_id=1, source_target_pairs={{0,8},{8,16},{16,24},{24,32},{32,40},{40,48},{48,56},{56,64},{64,7... | collective-permute-start | bytes 1179656 | tf_op jit(solution)/shard_map/ppermute | solution.py:13
  24.4 1.9 %collective-permute-start.5 = (bf16[2,256,384]{2,1,0:T(8,128)(2,1)S(1)}, bf16[2,256,384]{2,1,0:T(8,128)(2,1)}, u32[]{:S(2)}, u32[]{:S(2)}) collective-permute-start(bf16[2,256,384]{2,1,0:T(8,128)(2,1)S(1)} %collective-permute-done.4), channel_id=1, source_target_pairs={{8,0},{16,8},{24,16},{32,24},{40,32},{48,40},{56,48},{64,56},{72,6... | collective-permute-start | bytes 1179656 | tf_op jit(solution)/shard_map/ppermute | solution.py:13
  26.3 1.7 %compare_and_fusion = (pred[2,2]{1,0:T(4,128)(4,1)S(1)}, pred[2,2]{1,0:T(4,128)(4,1)S(1)}, pred[2,2]{1,0:T(4,128)(4,1)S(1)}, pred[2,2]{1,0:T(4,128)(4,1)S(1)}, p...) fusion(s32[2,64]{1,0:T(2,128)} %param.11, ...), kind=kLoop, calls=%fused_computation.161 | loop fusion | flops 72 | bytes 225 | tf_op jit(solution)/shard_map/and | solution.py:41
  28.0 1.4 concatenate.21
  29.4 0.8 copy.26
  30.1 5.7 %collective-permute-start.2 = (bf16[2,256,384]{2,1,0:T(8,128)(2,1)S(1)}, bf16[2,256,384]{2,1,0:T(8,128)(2,1)S(1)}, u32[]{:S(2)}, u32[]{:S(2)}) collective-permute-start(bf16[2,256,384]{2,1,0:T(8,128)(2,1)S(1)} %collective-permute-done.1), channel_id=1, source_target_pairs={{0,8},{8,16},{16,24},{24,32},{32,40},{40,48},{48,56},{56,64},{64,7... | collective-permute-start | bytes 1179656 | tf_op jit(solution)/shard_map/ppermute | solution.py:13
  36.0 1.1 constant_dynamic-update-slice_fusion
  37.1 1.9 %collective-permute-start.6 = (bf16[2,256,384]{2,1,0:T(8,128)(2,1)}, bf16[2,256,384]{2,1,0:T(8,128)(2,1)S(1)}, u32[]{:S(2)}, u32[]{:S(2)}) collective-permute-start(bf16[2,256,384]{2,1,0:T(8,128)(2,1)} %collective-permute-done.5), channel_id=1, source_target_pairs={{8,0},{16,8},{24,16},{32,24},{40,32},{48,40},{56,48},{64,56},{72,6... | collective-permute-start | bytes 1179656 | tf_op jit(solution)/shard_map/ppermute | solution.py:13
  39.1 1.5 collective-permute-done.2
  40.6 6.5 %collective-permute-start.3 = (bf16[2,256,384]{2,1,0:T(8,128)(2,1)S(1)}, bf16[2,256,384]{2,1,0:T(8,128)(2,1)S(1)}, u32[]{:S(2)}, u32[]{:S(2)}) collective-permute-start(bf16[2,256,384]{2,1,0:T(8,128)(2,1)S(1)} %collective-permute-done.2), channel_id=1, source_target_pairs={{0,8},{8,16},{16,24},{24,32},{32,40},{40,48},{48,56},{56,64},{64,7... | collective-permute-start | bytes 1179656 | tf_op jit(solution)/shard_map/ppermute | solution.py:13
  47.2 1.4 collective-permute-done.6
  48.5 1.9 %collective-permute-start.7 = (bf16[2,256,384]{2,1,0:T(8,128)(2,1)S(1)}, bf16[2,256,384]{2,1,0:T(8,128)(2,1)S(1)}, u32[]{:S(2)}, u32[]{:S(2)}) collective-permute-start(bf16[2,256,384]{2,1,0:T(8,128)(2,1)S(1)} %collective-permute-done.6), channel_id=1, source_target_pairs={{8,0},{16,8},{24,16},{32,24},{40,32},{48,40},{56,48},{64,56},{72,6... | collective-permute-start | bytes 1179656 | tf_op jit(solution)/shard_map/ppermute | solution.py:13
  50.5 1.3 collective-permute-done.3
  51.9 1.1 fusion.40
  53.1 6.6 %collective-permute-done.7 = bf16[2,256,384]{2,1,0:T(8,128)(2,1)S(1)} collective-permute-done((bf16[2,256,384]{2,1,0:T(8,128)(2,1)S(1)}, bf16[2,256,384]{2,1,0:T(8,128)(2,1)S(1)}, u32[]{:S(2)}, u32[]{:S(2)}) %collective-permute-start.7) | collective-permute-done | bytes 393248 | tf_op jit(solution)/shard_map/ppermute | solution.py:13
  59.9 0.6 fusion.80
  60.4 0.6 fusion.81
  61.1 0.6 fusion.82
  63.6 1.1 convolution_convert_fusion.5
  65.1 1.0 convolution_convert_fusion.6
  66.5 2.3 %convolution_convert_fusion.1 = bf16[256,384]{0,1:T(8,128)(2,1)S(1)} fusion(bf16[256,3072]{1,0:T(8,128)(2,1)} %all-gather.2.cloned.1.call-done, bf16[384,3072]{1,0:T(8,128)(2,1)S(1)} %copy-done), kind=kOutput, calls=%fused_computation.30 | convolution fusion | flops 604078080 | bytes 4128768 | tf_op jit(solution)/shard_map/dot_general | solution.py:71
  69.4 0.7 copy-done.11
  70.7 0.5 fusion.74
  71.6 0.7 copy-done.25
  72.7 1.2 copy-done.6
  73.9 0.7 fusion.8
  74.7 0.9 copy-done.4
  75.6 0.7 fusion.7
  76.3 0.9 copy-done.2
  77.3 0.7 fusion.6
  78.7 0.5 fusion.59
  79.8 1.4 fusion.79
  81.3 2.0 %pad_maximum_fusion = f32[2304,384]{0,1:T(8,128)} fusion(f32[2304,128]{0,1:T(8,128)S(1)} %fusion.59, f32[2304,128]{0,1:T(8,128)S(1)} %fusion.62, f32[2304,128]{0,1:T(8,128)S(1)} %fusion.65), kind=kLoop, calls=%fused_computation.19 | loop fusion | flops 1769472 | bytes 7077888 | tf_op jit(solution)/shard_map/concatenate | solution.py:110
  83.3 1.4 fusion.78
  84.6 2.0 %pad_maximum_fusion.1 = f32[2304,384]{0,1:T(8,128)} fusion(f32[2304,128]{0,1:T(8,128)S(1)} %fusion.68, f32[2304,128]{0,1:T(8,128)S(1)} %fusion.71, f32[2304,128]{0,1:T(8,128)S(1)} %fusion.74), kind=kLoop, calls=%fused_computation.20 | loop fusion | flops 1769472 | bytes 7077888 | tf_op jit(solution)/shard_map/concatenate | solution.py:111
  86.6 2.2 %convolution_convert_fusion = bf16[256,3072]{1,0:T(8,128)(2,1)} fusion(bf16[384,3072]{1,0:T(8,128)(2,1)S(1)} %copy-done, bf16[256,128]{0,1:T(8,128)(2,1)S(1)} %copy-done.22, bf16[256,128]{0,1:T(8,128)(2,1)S(1)} %copy-done.23, bf16[256,128]{0,1:T(8,128)(2,1)S(1)} %get-tuple-element.70), kind=kOutput, calls=%fused_computation.18 | convolution fusion | flops 605356032 | bytes 4128768 | tf_op jit(solution)/shard_map/dot_general | solution.py:67
  88.8 2.6 %copy.38 = bf16[256,3072]{0,1:T(8,128)(2,1)} copy(bf16[256,3072]{1,0:T(8,128)(2,1)} %convolution_convert_fusion) | data formatting | bytes 3145728
  91.4 1.1 slice_bitcast_fusion.19
  92.5 2.1 %slice_bitcast_fusion.11 = (f32[1,256,384]{1,2,0:T(8,128)S(1)}, f32[1,256,384]{1,2,0:T(8,128)S(1)}, f32[1,256,384]{1,2,0:T(8,128)S(1)}, f32[1,256,384]{1,2,0:T(8...) fusion(f32[2304,384]{0,1:T(8,128)} %pad_maximum_fusion), kind=kLoop, calls=%fused_computation.78 | loop fusion | bytes 5505024 | tf_op jit(solution)/shard_map/stack | solution.py:115
  94.6 1.1 slice_bitcast_fusion.18
  95.7 3.1 %collective-permute-start.12 = (bf16[2,256,384]{1,2,0:T(8,128)(2,1)S(1)}, bf16[2,256,384]{1,2,0:T(8,128)(2,1)S(1)}, u32[]{:S(2)}, u32[]{:S(2)}) collective-permute-start(bf16[2,256,384]{1,2,0:T(8,128)(2,1)S(1)} %pad_maximum_fusion.4), channel_id=1, source_target_pairs={{0,8},{8,16},{16,24},{24,32},{32,40},{40,48},{48,56},{56,64},{64,7... | collective-permute-start | bytes 1179656 | tf_op jit(solution)/shard_map/ppermute | solution.py:13
  98.9 1.9 %collective-permute-start.8 = (bf16[2,256,384]{1,2,0:T(8,128)(2,1)S(1)}, bf16[2,256,384]{1,2,0:T(8,128)(2,1)S(1)}, u32[]{:S(2)}, u32[]{:S(2)}) collective-permute-start(bf16[2,256,384]{1,2,0:T(8,128)(2,1)S(1)} %pad_maximum_fusion.3), channel_id=1, source_target_pairs={{8,0},{16,8},{24,16},{32,24},{40,32},{48,40},{56,48},{64,56},{72,6... | collective-permute-start | bytes 1179656 | tf_op jit(solution)/shard_map/ppermute | solution.py:13
  101.1 2.4 %collective-permute-done.12 = bf16[2,256,384]{1,2,0:T(8,128)(2,1)S(1)} collective-permute-done((bf16[2,256,384]{1,2,0:T(8,128)(2,1)S(1)}, bf16[2,256,384]{1,2,0:T(8,128)(2,1)S(1)}, u32[]{:S(2)}, u32[]{:S(2)}) %collective-permute-start.12) | collective-permute-done | bytes 393248 | tf_op jit(solution)/shard_map/ppermute | solution.py:13
  103.6 6.5 %collective-permute-start.13 = (bf16[2,256,384]{1,2,0:T(8,128)(2,1)S(1)}, bf16[2,256,384]{1,2,0:T(8,128)(2,1)S(1)}, u32[]{:S(2)}, u32[]{:S(2)}) collective-permute-start(bf16[2,256,384]{1,2,0:T(8,128)(2,1)S(1)} %fusion.20), channel_id=1, source_target_pairs={{0,8},{8,16},{16,24},{24,32},{32,40},{40,48},{48,56},{56,64},{64,7... | collective-permute-start | bytes 1179656 | tf_op jit(solution)/shard_map/ppermute | solution.py:13
  110.3 2.2 %collective-permute-start.9 = (bf16[2,256,384]{1,2,0:T(8,128)(2,1)S(1)}, bf16[2,256,384]{1,2,0:T(8,128)(2,1)S(1)}, u32[]{:S(2)}, u32[]{:S(2)}) collective-permute-start(bf16[2,256,384]{1,2,0:T(8,128)(2,1)S(1)} %fusion.17), channel_id=1, source_target_pairs={{8,0},{16,8},{24,16},{32,24},{40,32},{48,40},{56,48},{64,56},{72,6... | collective-permute-start | bytes 1179656 | tf_op jit(solution)/shard_map/ppermute | solution.py:13
  112.4 2.4 %collective-permute-done.13 = bf16[2,256,384]{1,2,0:T(8,128)(2,1)S(1)} collective-permute-done((bf16[2,256,384]{1,2,0:T(8,128)(2,1)S(1)}, bf16[2,256,384]{1,2,0:T(8,128)(2,1)S(1)}, u32[]{:S(2)}, u32[]{:S(2)}) %collective-permute-start.13) | collective-permute-done | bytes 393248 | tf_op jit(solution)/shard_map/ppermute | solution.py:13
  114.9 6.5 %collective-permute-start.14 = (bf16[2,256,384]{1,2,0:T(8,128)(2,1)S(1)}, bf16[2,256,384]{1,2,0:T(8,128)(2,1)S(1)}, u32[]{:S(2)}, u32[]{:S(2)}) collective-permute-start(bf16[2,256,384]{1,2,0:T(8,128)(2,1)S(1)} %fusion.21), channel_id=1, source_target_pairs={{0,8},{8,16},{16,24},{24,32},{32,40},{40,48},{48,56},{56,64},{64,7... | collective-permute-start | bytes 1179656 | tf_op jit(solution)/shard_map/ppermute | solution.py:13
  121.8 1.9 %collective-permute-start.10 = (bf16[2,256,384]{1,2,0:T(8,128)(2,1)S(1)}, bf16[2,256,384]{1,2,0:T(8,128)(2,1)S(1)}, u32[]{:S(2)}, u32[]{:S(2)}) collective-permute-start(bf16[2,256,384]{1,2,0:T(8,128)(2,1)S(1)} %fusion.18), channel_id=1, source_target_pairs={{8,0},{16,8},{24,16},{32,24},{40,32},{48,40},{56,48},{64,56},{72,6... | collective-permute-start | bytes 1179656 | tf_op jit(solution)/shard_map/ppermute | solution.py:13
  124.2 2.0 %collective-permute-done.14 = bf16[2,256,384]{1,2,0:T(8,128)(2,1)S(1)} collective-permute-done((bf16[2,256,384]{1,2,0:T(8,128)(2,1)S(1)}, bf16[2,256,384]{1,2,0:T(8,128)(2,1)S(1)}, u32[]{:S(2)}, u32[]{:S(2)}) %collective-permute-start.14) | collective-permute-done | bytes 393248 | tf_op jit(solution)/shard_map/ppermute | solution.py:13
  126.1 0.8 fusion.22
  127.0 6.5 %collective-permute-start.15 = (bf16[2,256,384]{1,2,0:T(8,128)(2,1)}, bf16[2,256,384]{1,2,0:T(8,128)(2,1)}, u32[]{:S(2)}, u32[]{:S(2)}) collective-permute-start(bf16[2,256,384]{1,2,0:T(8,128)(2,1)} %fusion.22), channel_id=1, source_target_pairs={{0,8},{8,16},{16,24},{24,32},{32,40},{40,48},{48,56},{56,64},{64,7... | collective-permute-start | bytes 1179656 | tf_op jit(solution)/shard_map/ppermute | solution.py:13
  133.5 0.9 fusion.19
  134.3 1.9 %collective-permute-start.11 = (bf16[2,256,384]{1,2,0:T(8,128)(2,1)}, bf16[2,256,384]{1,2,0:T(8,128)(2,1)}, u32[]{:S(2)}, u32[]{:S(2)}) collective-permute-start(bf16[2,256,384]{1,2,0:T(8,128)(2,1)} %fusion.19), channel_id=1, source_target_pairs={{8,0},{16,8},{24,16},{32,24},{40,32},{48,40},{56,48},{64,56},{72,6... | collective-permute-start | bytes 1179656 | tf_op jit(solution)/shard_map/ppermute | solution.py:13
  137.1 0.8 copy.31
  137.9 0.6 collective-permute-done.15
  138.5 7.4 %collective-permute-done.11 = bf16[2,256,384]{1,2,0:T(8,128)(2,1)} collective-permute-done((bf16[2,256,384]{1,2,0:T(8,128)(2,1)}, bf16[2,256,384]{1,2,0:T(8,128)(2,1)}, u32[]{:S(2)}, u32[]{:S(2)}) %collective-permute-start.11) | collective-permute-done | bytes 393248 | tf_op jit(solution)/shard_map/ppermute | solution.py:13
  145.9 1.2 fusion.16
  147.1 0.8 copy.33
  147.9 0.8 copy.32
  148.8 1.7 %copy.39 = bf16[256,384]{1,0:T(8,128)(2,1)} copy(bf16[256,384]{0,1:T(8,128)(2,1)} %bitcast.148) | data formatting | bytes 393216
  (100 shorter events, 8.9 us)
Async XLA Ops:
  7.2 59.4 %copy-start = (bf16[384,3072]{1,0:T(8,128)(2,1)S(1)}, bf16[384,3072]{1,0:T(8,128)(2,1)}, u32[]{:S(2)}) copy-start(bf16[384,3072]{1,0:T(8,128)(2,1)} %param.10) | copy-start | bytes 7077892
  7.2 59.3 %all-gather.2.cloned.1.call-start = ((), (), s32[]{:S(2)}) async-start(), calls=%async_computation.1 | async-start | bytes 1769472 | tf_op jit(solution)/shard_map/all_gather | solution.py:72
  9.2 8.7 %collective-permute-start = (bf16[2,256,384]{2,1,0:T(8,128)(2,1)}, bf16[2,256,384]{2,1,0:T(8,128)(2,1)S(1)}, u32[]{:S(2)}, u32[]{:S(2)}) collective-permute-start(bf16[2,256,384]{2,1,0:T(8,128)(2,1)} %pad_maximum_fusion.2), channel_id=1, source_target_pairs={{0,8},{8,16},{16,24},{24,32},{32,40},{40,48},{48,56},{56,64},{64,7... | collective-permute-start | bytes 1179656 | tf_op jit(solution)/shard_map/ppermute | solution.py:13
  12.9 11.5 %collective-permute-start.4 = (bf16[2,256,384]{2,1,0:T(8,128)(2,1)}, bf16[2,256,384]{2,1,0:T(8,128)(2,1)S(1)}, u32[]{:S(2)}, u32[]{:S(2)}) collective-permute-start(bf16[2,256,384]{2,1,0:T(8,128)(2,1)} %pad_maximum_fusion.2), channel_id=1, source_target_pairs={{8,0},{16,8},{24,16},{32,24},{40,32},{48,40},{56,48},{64,56},{72,6... | collective-permute-start | bytes 1179656 | tf_op jit(solution)/shard_map/ppermute | solution.py:13
  17.9 12.3 %collective-permute-start.1 = (bf16[2,256,384]{2,1,0:T(8,128)(2,1)S(1)}, bf16[2,256,384]{2,1,0:T(8,128)(2,1)S(1)}, u32[]{:S(2)}, u32[]{:S(2)}) collective-permute-start(bf16[2,256,384]{2,1,0:T(8,128)(2,1)S(1)} %collective-permute-done), channel_id=1, source_target_pairs={{0,8},{8,16},{16,24},{24,32},{32,40},{40,48},{48,56},{56,64},{64,7... | collective-permute-start | bytes 1179656 | tf_op jit(solution)/shard_map/ppermute | solution.py:13
  24.3 124.5 %reduce-scatter.4.cloned.1.call-start = ((), (), s32[]{:S(2)}) async-start(), calls=%async_computation.2 | async-start | bytes 1769472
  24.4 12.7 %collective-permute-start.5 = (bf16[2,256,384]{2,1,0:T(8,128)(2,1)S(1)}, bf16[2,256,384]{2,1,0:T(8,128)(2,1)}, u32[]{:S(2)}, u32[]{:S(2)}) collective-permute-start(bf16[2,256,384]{2,1,0:T(8,128)(2,1)S(1)} %collective-permute-done.4), channel_id=1, source_target_pairs={{8,0},{16,8},{24,16},{32,24},{40,32},{48,40},{56,48},{64,56},{72,6... | collective-permute-start | bytes 1179656 | tf_op jit(solution)/shard_map/ppermute | solution.py:13
  30.1 10.5 %collective-permute-start.2 = (bf16[2,256,384]{2,1,0:T(8,128)(2,1)S(1)}, bf16[2,256,384]{2,1,0:T(8,128)(2,1)S(1)}, u32[]{:S(2)}, u32[]{:S(2)}) collective-permute-start(bf16[2,256,384]{2,1,0:T(8,128)(2,1)S(1)} %collective-permute-done.1), channel_id=1, source_target_pairs={{0,8},{8,16},{16,24},{24,32},{32,40},{40,48},{48,56},{56,64},{64,7... | collective-permute-start | bytes 1179656 | tf_op jit(solution)/shard_map/ppermute | solution.py:13
  37.1 11.4 %collective-permute-start.6 = (bf16[2,256,384]{2,1,0:T(8,128)(2,1)}, bf16[2,256,384]{2,1,0:T(8,128)(2,1)S(1)}, u32[]{:S(2)}, u32[]{:S(2)}) collective-permute-start(bf16[2,256,384]{2,1,0:T(8,128)(2,1)} %collective-permute-done.5), channel_id=1, source_target_pairs={{8,0},{16,8},{24,16},{32,24},{40,32},{48,40},{56,48},{64,56},{72,6... | collective-permute-start | bytes 1179656 | tf_op jit(solution)/shard_map/ppermute | solution.py:13
  40.6 11.2 %collective-permute-start.3 = (bf16[2,256,384]{2,1,0:T(8,128)(2,1)S(1)}, bf16[2,256,384]{2,1,0:T(8,128)(2,1)S(1)}, u32[]{:S(2)}, u32[]{:S(2)}) collective-permute-start(bf16[2,256,384]{2,1,0:T(8,128)(2,1)S(1)} %collective-permute-done.2), channel_id=1, source_target_pairs={{0,8},{8,16},{16,24},{24,32},{32,40},{40,48},{48,56},{56,64},{64,7... | collective-permute-start | bytes 1179656 | tf_op jit(solution)/shard_map/ppermute | solution.py:13
  48.5 11.2 %collective-permute-start.7 = (bf16[2,256,384]{2,1,0:T(8,128)(2,1)S(1)}, bf16[2,256,384]{2,1,0:T(8,128)(2,1)S(1)}, u32[]{:S(2)}, u32[]{:S(2)}) collective-permute-start(bf16[2,256,384]{2,1,0:T(8,128)(2,1)S(1)} %collective-permute-done.6), channel_id=1, source_target_pairs={{8,0},{16,8},{24,16},{32,24},{40,32},{48,40},{56,48},{64,56},{72,6... | collective-permute-start | bytes 1179656 | tf_op jit(solution)/shard_map/ppermute | solution.py:13
  51.9 8.0 %copy-start.20 = (bf16[256,384]{1,0:T(8,128)(2,1)S(1)}, bf16[256,384]{1,0:T(8,128)(2,1)}, u32[]{:S(2)}) copy-start(bf16[256,384]{1,0:T(8,128)(2,1)} %param.6) | copy-start | bytes 589828
  59.8 1.3 copy-start.12
  59.8 5.2 %copy-start.24 = (bf16[2304,384]{1,0:T(8,128)(2,1)}, bf16[2304,384]{1,0:T(8,128)(2,1)S(1)}, u32[]{:S(2)}) copy-start(bf16[2304,384]{1,0:T(8,128)(2,1)S(1)} %get-tuple-element.39) | copy-start | bytes 5308420
  60.4 2.4 %copy-start.5 = (f32[256,2304]{0,1:T(8,128)}, f32[256,2304]{0,1:T(8,128)S(1)}, u32[]{:S(2)}) copy-start(f32[256,2304]{0,1:T(8,128)S(1)} %get-tuple-element.65) | copy-start | bytes 7077892
  61.1 3.6 %copy-start.3 = (f32[256,2304]{0,1:T(8,128)}, f32[256,2304]{0,1:T(8,128)S(1)}, u32[]{:S(2)}) copy-start(f32[256,2304]{0,1:T(8,128)S(1)} %get-tuple-element.67) | copy-start | bytes 7077892
  61.7 4.5 %copy-start.1 = (f32[256,2304]{0,1:T(8,128)}, f32[256,2304]{0,1:T(8,128)S(1)}, u32[]{:S(2)}) copy-start(f32[256,2304]{0,1:T(8,128)S(1)} %get-tuple-element.69) | copy-start | bytes 7077892
  62.1 1.1 copy-start.28
  62.5 2.2 %copy-start.26 = (f32[256]{0:T(256)}, f32[256]{0:T(256)S(1)}, u32[]{:S(2)}) copy-start(f32[256]{0:T(256)S(1)} %fusion.12) | copy-start | bytes 3076
  63.6 1.5 copy-start.8
  65.1 1.0 copy-start.10
  66.5 2.3 %copy-start.9 = (bf16[256,2304]{0,1:T(8,128)(2,1)S(1)}, bf16[256,2304]{0,1:T(8,128)(2,1)}, u32[]{:S(2)}) copy-start(bf16[256,2304]{0,1:T(8,128)(2,1)} %copy-done.8) | copy-start | bytes 3538948
  68.9 1.3 copy-start.11
  70.7 0.8 copy-start.22
  70.7 0.9 copy-start.23
  70.7 1.5 copy-start.25
  72.2 1.7 %copy-start.6 = (f32[256,2304]{0,1:T(8,128)S(1)}, f32[256,2304]{0,1:T(8,128)}, u32[]{:S(2)}) copy-start(f32[256,2304]{0,1:T(8,128)} %copy-done.5) | copy-start | bytes 7077892
  72.3 1.7 %copy-start.29 = (f32[256]{0:T(256)S(1)}, f32[256]{0:T(256)}, u32[]{:S(2)}) copy-start(f32[256]{0:T(256)} %copy-done.28) | copy-start | bytes 3076
  73.9 1.7 %copy-start.4 = (f32[256,2304]{0,1:T(8,128)S(1)}, f32[256,2304]{0,1:T(8,128)}, u32[]{:S(2)}) copy-start(f32[256,2304]{0,1:T(8,128)} %copy-done.3) | copy-start | bytes 7077892
  73.9 1.7 %copy-start.27 = (f32[256]{0:T(256)S(1)}, f32[256]{0:T(256)}, u32[]{:S(2)}) copy-start(f32[256]{0:T(256)} %copy-done.26) | copy-start | bytes 3076
  74.6 4.1 %copy-start.14 = (bf16[256,2304]{0,1:T(8,128)(2,1)}, bf16[256,2304]{0,1:T(8,128)(2,1)S(1)}, u32[]{:S(2)}) copy-start(bf16[256,2304]{0,1:T(8,128)(2,1)S(1)} %fusion.8) | copy-start | bytes 3538948
  75.6 1.7 %copy-start.2 = (f32[256,2304]{0,1:T(8,128)S(1)}, f32[256,2304]{0,1:T(8,128)}, u32[]{:S(2)}) copy-start(f32[256,2304]{0,1:T(8,128)} %copy-done.1) | copy-start | bytes 7077892
  76.3 3.0 %copy-start.16 = (bf16[256,2304]{0,1:T(8,128)(2,1)}, bf16[256,2304]{0,1:T(8,128)(2,1)S(1)}, u32[]{:S(2)}) copy-start(bf16[256,2304]{0,1:T(8,128)(2,1)S(1)} %fusion.7) | copy-start | bytes 3538948
  77.3 0.9 copy-start.21
  78.2 1.1 copy-start.18
  92.4 8.4 %copy-start.7 = (f32[2304,384]{0,1:T(8,128)S(1)}, f32[2304,384]{0,1:T(8,128)}, u32[]{:S(2)}) copy-start(f32[2304,384]{0,1:T(8,128)} %pad_maximum_fusion.1) | copy-start | bytes 10616836
  95.7 7.9 %collective-permute-start.12 = (bf16[2,256,384]{1,2,0:T(8,128)(2,1)S(1)}, bf16[2,256,384]{1,2,0:T(8,128)(2,1)S(1)}, u32[]{:S(2)}, u32[]{:S(2)}) collective-permute-start(bf16[2,256,384]{1,2,0:T(8,128)(2,1)S(1)} %pad_maximum_fusion.4), channel_id=1, source_target_pairs={{0,8},{8,16},{16,24},{24,32},{32,40},{40,48},{48,56},{56,64},{64,7... | collective-permute-start | bytes 1179656 | tf_op jit(solution)/shard_map/ppermute | solution.py:13
  98.9 11.3 %collective-permute-start.8 = (bf16[2,256,384]{1,2,0:T(8,128)(2,1)S(1)}, bf16[2,256,384]{1,2,0:T(8,128)(2,1)S(1)}, u32[]{:S(2)}, u32[]{:S(2)}) collective-permute-start(bf16[2,256,384]{1,2,0:T(8,128)(2,1)S(1)} %pad_maximum_fusion.3), channel_id=1, source_target_pairs={{8,0},{16,8},{24,16},{32,24},{40,32},{48,40},{56,48},{64,56},{72,6... | collective-permute-start | bytes 1179656 | tf_op jit(solution)/shard_map/ppermute | solution.py:13
  103.6 11.2 %collective-permute-start.13 = (bf16[2,256,384]{1,2,0:T(8,128)(2,1)S(1)}, bf16[2,256,384]{1,2,0:T(8,128)(2,1)S(1)}, u32[]{:S(2)}, u32[]{:S(2)}) collective-permute-start(bf16[2,256,384]{1,2,0:T(8,128)(2,1)S(1)} %fusion.20), channel_id=1, source_target_pairs={{0,8},{8,16},{16,24},{24,32},{32,40},{40,48},{48,56},{56,64},{64,7... | collective-permute-start | bytes 1179656 | tf_op jit(solution)/shard_map/ppermute | solution.py:13
  110.2 13.5 %copy-start.13 = (bf16[2304,384]{1,0:T(8,128)(2,1)S(1)}, bf16[2304,384]{1,0:T(8,128)(2,1)}, u32[]{:S(2)}) copy-start(bf16[2304,384]{1,0:T(8,128)(2,1)} %copy-done.12) | copy-start | bytes 5308420
  110.2 13.5 %copy-start.19 = (bf16[256,2304]{0,1:T(8,128)(2,1)S(1)}, bf16[256,2304]{0,1:T(8,128)(2,1)}, u32[]{:S(2)}) copy-start(bf16[256,2304]{0,1:T(8,128)(2,1)} %copy-done.18) | copy-start | bytes 3538948
  110.3 11.5 %collective-permute-start.9 = (bf16[2,256,384]{1,2,0:T(8,128)(2,1)S(1)}, bf16[2,256,384]{1,2,0:T(8,128)(2,1)S(1)}, u32[]{:S(2)}, u32[]{:S(2)}) collective-permute-start(bf16[2,256,384]{1,2,0:T(8,128)(2,1)S(1)} %fusion.17), channel_id=1, source_target_pairs={{8,0},{16,8},{24,16},{32,24},{40,32},{48,40},{56,48},{64,56},{72,6... | collective-permute-start | bytes 1179656 | tf_op jit(solution)/shard_map/ppermute | solution.py:13
  114.9 11.2 %collective-permute-start.14 = (bf16[2,256,384]{1,2,0:T(8,128)(2,1)S(1)}, bf16[2,256,384]{1,2,0:T(8,128)(2,1)S(1)}, u32[]{:S(2)}, u32[]{:S(2)}) collective-permute-start(bf16[2,256,384]{1,2,0:T(8,128)(2,1)S(1)} %fusion.21), channel_id=1, source_target_pairs={{0,8},{8,16},{16,24},{24,32},{32,40},{40,48},{48,56},{56,64},{64,7... | collective-permute-start | bytes 1179656 | tf_op jit(solution)/shard_map/ppermute | solution.py:13
  121.8 11.6 %collective-permute-start.10 = (bf16[2,256,384]{1,2,0:T(8,128)(2,1)S(1)}, bf16[2,256,384]{1,2,0:T(8,128)(2,1)S(1)}, u32[]{:S(2)}, u32[]{:S(2)}) collective-permute-start(bf16[2,256,384]{1,2,0:T(8,128)(2,1)S(1)} %fusion.18), channel_id=1, source_target_pairs={{8,0},{16,8},{24,16},{32,24},{40,32},{48,40},{56,48},{64,56},{72,6... | collective-permute-start | bytes 1179656 | tf_op jit(solution)/shard_map/ppermute | solution.py:13
  124.2 12.1 %copy-start.17 = (bf16[256,2304]{0,1:T(8,128)(2,1)S(1)}, bf16[256,2304]{0,1:T(8,128)(2,1)}, u32[]{:S(2)}) copy-start(bf16[256,2304]{0,1:T(8,128)(2,1)} %copy-done.16) | copy-start | bytes 3538948
  127.0 11.5 %collective-permute-start.15 = (bf16[2,256,384]{1,2,0:T(8,128)(2,1)}, bf16[2,256,384]{1,2,0:T(8,128)(2,1)}, u32[]{:S(2)}, u32[]{:S(2)}) collective-permute-start(bf16[2,256,384]{1,2,0:T(8,128)(2,1)} %fusion.22), channel_id=1, source_target_pairs={{0,8},{8,16},{16,24},{24,32},{32,40},{40,48},{48,56},{56,64},{64,7... | collective-permute-start | bytes 1179656 | tf_op jit(solution)/shard_map/ppermute | solution.py:13
  133.5 3.2 %copy-start.15 = (bf16[256,2304]{0,1:T(8,128)(2,1)S(1)}, bf16[256,2304]{0,1:T(8,128)(2,1)}, u32[]{:S(2)}) copy-start(bf16[256,2304]{0,1:T(8,128)(2,1)} %copy-done.14) | copy-start | bytes 3538948
  134.3 11.5 %collective-permute-start.11 = (bf16[2,256,384]{1,2,0:T(8,128)(2,1)}, bf16[2,256,384]{1,2,0:T(8,128)(2,1)}, u32[]{:S(2)}, u32[]{:S(2)}) collective-permute-start(bf16[2,256,384]{1,2,0:T(8,128)(2,1)} %fusion.19), channel_id=1, source_target_pairs={{8,0},{16,8},{24,16},{32,24},{40,32},{48,40},{56,48},{64,56},{72,6... | collective-permute-start | bytes 1179656 | tf_op jit(solution)/shard_map/ppermute | solution.py:13
Sparse Core Ops, SparseCore 0:
  24.4 36.4 all-gather.1
  91.5 38.5 reduce-scatter.3
where the time goes:
time: 158 us; the launch traced here: 157 us
  starting transfers between devices  60.6 us (38%)
  waiting for transfers between devices  28.9 us (18%)
  local copies, waits for them, and re-layouts  21.7 us (14%)
  other arithmetic  16.1 us (10%)
  matrix products  15.2 us (10%)
  between operations  14.7 us (9%)
    ppermute x16, starting transfers between devices, from_behind(): lax.ppermute(value, axis, [(source, source + steps) for source in range(i...  60.5 us
    ppermute x16, waiting for transfers between devices, from_behind(): lax.ppermute(value, axis, [(source, source + steps) for source in range(i...  28.9 us
    unnamed x76, local copies, waits for them, and re-layouts  15 us
    another operation x4, local copies, waits for them, and re-layouts, local(): jnp.stack([dk_all[lower_row:lower_row + row_count], dv_all[lower_row:lowe...  4.47 us
    another operation x3, other arithmetic  4.03 us
  transfers between devices with their start and end apart: 18, of which 11 were waited for; matrix products, arithmetic and copies ran while one was open for 15% of the time, Pallas kernels for 0%

commit v1 on v0

v1 whole, which is shorter than its diff:
```python
import functools

import jax
import jax.numpy as jnp
from jax import lax
from jax.experimental import pallas as pl
from jax.experimental.pallas import tpu as pltpu
from jax.sharding import PartitionSpec as P


HEAD_DIM = 128
BLOCK = 128
PARTS = 9
FAR = 3
BF16 = jnp.bfloat16
F32 = jnp.float32
VMEM_LIMIT = 40 * 1024 * 1024


def core_swap(value):
    count = lax.axis_size("tm")
    return lax.ppermute(value, "tm", [(s, s ^ 1) for s in range(count)])


def chip_step(value, sign):
    count = lax.axis_size("tm")
    pairs = [(s, (s + (2 * sign if s % 2 == 0 else -2 * sign)) % count) for s in range(count)]
    return lax.ppermute(value, "tm", pairs)


def ring_step(value):
    groups, count = lax.axis_size("tm"), lax.axis_size("head")
    pairs = [
        (t * count + z, t * count + (z + (1 if t % 2 == 0 else -1)) % count)
        for t in range(groups)
        for z in range(count)
    ]
    return lax.ppermute(value, ("tm", "head"), pairs)


def wide(x):
    return x.astype(F32)


def contract(left, right, left_dim, right_dim):
    return lax.dot_general(
        left, right, (((left_dim,), (right_dim,)), ((), ())), preferred_element_type=F32
    )


def place():
    tm = lax.axis_index("tm")
    core = lax.rem(tm, 2)
    return tm, core, lax.axis_index("head"), 1 - 2 * core


def part_groups():
    tm, core, _, way = place()
    chip = lax.div(tm, 2)
    back2, back1 = 2 * (chip - 2 * way), 2 * (chip - way)
    ahead2, ahead1 = 2 * (chip + 2 * way), 2 * (chip + way)
    other = 1 - core
    return [
        back2 + core,
        back2 + other,
        ahead2 + core,
        back1 + core,
        back1 + other,
        ahead1 + other,
        ahead1 + core,
        tm,
        2 * chip + other,
    ]


def pack_kernel(own_k, own_v, own_d, sib_k, sib_v, sib_d, kv_out, d_out, sems):
    rows = own_k.shape[0]
    copies = []
    for i, (source, target, at) in enumerate(
        (
            (own_k, kv_out, 0),
            (own_v, kv_out, 1),
            (sib_k, kv_out, 2),
            (sib_v, kv_out, 3),
            (own_d, d_out, 0),
            (sib_d, d_out, 1),
        )
    ):
        copies.append(
            pltpu.make_async_copy(source, target.at[pl.ds(at * rows, rows), :], sems.at[i])
        )
    for copy in copies:
        copy.start()
    for copy in copies:
        copy.wait()


def forward_kernel(scale, mask, query, r2, s2, r1, s1, both, weight_any, *refs):
    probs_out, attn_out, keep_out, send_out, mine_out, score_buf, attn_buf, weight, sem = refs
    head = pl.program_id(0)
    rows = query.shape[0]
    half = rows // 2
    cols = attn_buf.shape[1]
    blocks = rows // BLOCK
    count = weight.shape[1] // cols
    _, core, z, way = place()
    tm_count = lax.axis_size("tm")
    parts = [(r2, 0), (r2, 1), (s2, 0), (r1, 0), (r1, 1), (s1, 0), (s1, 1), (both, 0), (both, 1)]
    copy = pltpu.make_async_copy(weight_any, weight, sem)

    @pl.when(head == 0)
    def _():
        copy.start()

    q = query[...]
    top = None
    for p, ((part, at), group) in enumerate(zip(parts, part_groups())):
        inside = (group >= 0) & (group < tm_count)
        first = lax.clamp(0, group, tm_count - 1) * blocks
        keys = part[2 * at * rows : (2 * at + 1) * rows, :]
        scores = contract(keys, q, 1, 1) * scale
        for b in range(blocks):
            lanes = []
            for a in range(blocks):
                allowed = inside & (mask[a, first + b] == 1)
                lanes.append(jnp.full((1, BLOCK), jnp.where(allowed, 0.0, -jnp.inf), F32))
            piece = scores[b * BLOCK : (b + 1) * BLOCK] + jnp.concatenate(lanes, 1)
            score_buf[p * rows + b * BLOCK : p * rows + (b + 1) * BLOCK, :] = piece
            here = jnp.max(piece, axis=0, keepdims=True)
            top = here if top is None else jnp.maximum(top, here)
    total = None
    for p in range(PARTS):
        expo = jnp.exp(score_buf[p * rows : (p + 1) * rows, :] - top)
        score_buf[p * rows : (p + 1) * rows, :] = expo
        here = jnp.sum(expo, axis=0, keepdims=True)
        total = here if total is None else total + here
    inverse = 1.0 / total
    acc = None
    for p, (part, at) in enumerate(parts):
        weights = (score_buf[p * rows : (p + 1) * rows, :] * inverse).astype(BF16)
        probs_out[0, p * rows : (p + 1) * rows, :] = weights
        here = contract(part[(2 * at + 1) * rows : 2 * (at + 1) * rows, :], weights, 0, 0)
        acc = here if acc is None else acc + here
    attn_out[...] = acc.astype(BF16)
    attn_buf[:, pl.ds(pl.multiple_of(head * HEAD_DIM, HEAD_DIM), HEAD_DIM)] = acc.T.astype(BF16)

    @pl.when(head == pl.num_programs(0) - 1)
    def _():
        copy.wait()
        attn = attn_buf[...]

        def share(left, d):
            start = pl.multiple_of(lax.rem(z + d + count, count) * cols, HEAD_DIM)
            return contract(left, weight[:, pl.ds(start, cols)], 1, 0)

        mine_out[...] = share(attn, 0)
        for k in range(1, 4):
            keep_out[(k - 1) * rows : k * rows, :] = share(attn, way * k)
            send_out[(k - 1) * rows : k * rows, :] = share(attn, -way * k).astype(BF16)
        keep_rows = attn_buf[pl.ds(pl.multiple_of(core * half, half), half), :]
        send_rows = attn_buf[pl.ds(pl.multiple_of((1 - core) * half, half), half), :]
        keep_out[3 * rows :, :] = share(keep_rows, 4)
        send_out[3 * rows :, :] = share(send_rows, 4).astype(BF16)


def differentiate(scale, q, grad, attn, probs, parts):
    rows = q.shape[0]
    delta = jnp.sum(wide(grad).T * wide(attn), axis=0, keepdims=True)
    acc = None
    for p, (part, at, out, to) in enumerate(parts):
        keys, vals = 2 * at * rows, (2 * at + 1) * rows
        weights = probs[0, p * rows : (p + 1) * rows, :]
        out[(2 * to + 1) * rows : (2 * to + 2) * rows, :] = contract(weights, grad, 1, 0).astype(BF16)
        d_probs = contract(part[vals : vals + rows, :], grad, 1, 1)
        d_scores = (scale * wide(weights) * (d_probs - delta)).astype(BF16)
        out[2 * to * rows : (2 * to + 1) * rows, :] = contract(d_scores, q, 1, 0).astype(BF16)
        here = contract(part[keys : keys + rows, :], d_scores, 0, 0)
        acc = here if acc is None else acc + here
    return acc


def backward_far_kernel(scale, query, attn, probs, weight, r2, s2, *refs):
    own, a1, a2, a3, a4, b1, b2, b3, b4 = refs[:9]
    dq_out, grad_out, r2_out, s2_out, last = refs[9:]
    head = pl.program_id(0)
    rows, cols = grad_out.shape
    half = rows // 2
    count = weight.shape[1] // cols

    @pl.when(head == 0)
    def _():
        _, core, z, way = place()

        def term(piece, d):
            start = pl.multiple_of(lax.rem(z + d + count, count) * cols, HEAD_DIM)
            return contract(piece, weight[:, pl.ds(start, cols)], 1, 1)

        last[pl.ds(pl.multiple_of(core * half, half), half), :] = a4[:half, :]
        last[pl.ds(pl.multiple_of((1 - core) * half, half), half), :] = b4[...]
        acc = term(own[...], 0)
        for k, (a, b) in enumerate(((a1, b1), (a2, b2), (a3, b3))):
            acc += term(a[...], -way * (k + 1)) + term(b[...], way * (k + 1))
        acc += term(last[...], 4)
        grad_out[...] = acc.astype(BF16)

    grad = grad_out[:, pl.ds(pl.multiple_of(head * HEAD_DIM, HEAD_DIM), HEAD_DIM)]
    parts = [(r2, 0, r2_out, 0), (r2, 1, r2_out, 1), (s2, 0, s2_out, 0)]
    dq_out[...] = differentiate(scale, query[...], grad, attn[...], probs, parts)


def backward_near_kernel(scale, query, attn, probs, grad, dq_far, r1, s1, both, *refs):
    dq_out, r1_out, s1_out, both_out = refs
    parts = [(r, at, o, at) for r, o in ((r1, r1_out), (s1, s1_out), (both, both_out)) for at in (0, 1)]
    acc = differentiate(scale, query[...], grad[...], attn[...], probs, parts)
    dq_out[...] = (acc + dq_far[...]).T.astype(BF16)


def by_head(rows, at=0):
    return pl.BlockSpec((rows, HEAD_DIM), lambda h, *_: (at, h))


def by_head_rows(cols):
    return pl.BlockSpec((HEAD_DIM, cols), lambda h, *_: (h, 0))


def whole(rows, cols, at=0):
    return pl.BlockSpec((rows, cols), lambda h, *_: (at, 0))


def local(query_act, key_act, value_act, d_output, out_weight, block_mask):
    rows, cols = query_act.shape
    half = rows // 2
    scale = HEAD_DIM ** (-0.5)
    core = lax.axis_index("tm") % 2
    heads = cols // HEAD_DIM
    shape = jax.ShapeDtypeStruct
    vmem = pl.BlockSpec(memory_space=pltpu.VMEM)
    anywhere = pl.BlockSpec(memory_space=pl.ANY)
    limits = pltpu.CompilerParams(vmem_limit_bytes=VMEM_LIMIT)

    sib_k = core_swap(key_act)
    sib_v = core_swap(value_act)
    sib_d = core_swap(d_output)
    both, d_both = pl.pallas_call(
        pack_kernel,
        in_specs=[anywhere] * 6,
        out_specs=[vmem] * 2,
        out_shape=[shape((4 * rows, cols), BF16), shape((2 * rows, cols), BF16)],
        scratch_shapes=[pltpu.SemaphoreType.DMA((6,))],
        name="pack",
    )(key_act, value_act, d_output, sib_k, sib_v, sib_d)

    r1 = chip_step(both, 1)
    a1 = ring_step(d_both)
    a2 = ring_step(a1)
    r2 = chip_step(r1, 1)
    s1 = core_swap(r1)
    a3 = ring_step(a2)
    s2 = core_swap(r2)
    rest = jnp.where(
        core == 0,
        jnp.concatenate([a3[:half], a3[rows : rows + half]], 0),
        jnp.concatenate([a3[half:rows], a3[rows + half :]], 0),
    )
    a4 = ring_step(rest)
    b1 = core_swap(a1)
    b2 = core_swap(a2)
    b3 = core_swap(a3)
    b4 = core_swap(a4)

    probs, attn, keep, send, mine = pl.pallas_call(
        functools.partial(forward_kernel, scale),
        grid_spec=pltpu.PrefetchScalarGridSpec(
            num_scalar_prefetch=1,
            grid=(heads,),
            in_specs=[
                by_head(rows),
                by_head(4 * rows),
                by_head(2 * rows, 1),
                by_head(4 * rows),
                by_head(4 * rows),
                by_head(4 * rows),
                anywhere,
            ],
            out_specs=[
                pl.BlockSpec((1, PARTS * rows, rows), lambda h, *_: (h, 0, 0)),
                by_head_rows(rows),
                whole(3 * rows + half, cols),
                whole(3 * rows + half, cols),
                whole(rows, cols),
            ],
            scratch_shapes=[
                pltpu.VMEM((PARTS * rows, rows), F32),
                pltpu.VMEM((rows, cols), BF16),
                pltpu.VMEM(out_weight.shape, BF16),
                pltpu.SemaphoreType.DMA,
            ],
        ),
        out_shape=[
            shape((heads, PARTS * rows, rows), BF16),
            shape((cols, rows), BF16),
            shape((3 * rows + half, cols), F32),
            shape((3 * rows + half, cols), BF16),
            shape((rows, cols), F32),
        ],
        compiler_params=limits,
        cost_estimate=pl.CostEstimate(
            flops=4_000_000_000, bytes_accessed=12_000_000, transcendentals=1_800_000
        ),
        name="attend",
    )(block_mask, query_act, r2, s2, r1, s1, both, out_weight)

    other = core_swap(send)
    moved = ring_step(jnp.concatenate([keep[3 * rows :].astype(BF16), other[3 * rows :]], 0))
    in_half = (jnp.arange(rows) // half == core)[:, None]

    def spread(x):
        return jnp.where(in_half, jnp.concatenate([x, x], 0), 0.0)

    moved = jnp.concatenate([spread(wide(moved[:half])), spread(wide(moved[half:]))], 0)
    for k in (3, 2, 1):
        at = slice((k - 1) * rows, k * rows)
        moved = jnp.concatenate([keep[at] + moved[:rows], wide(other[at]) + moved[rows:]], 0)
        moved = wide(ring_step(moved.astype(BF16)))
    arrived = moved.astype(BF16)
    output = (mine + wide(arrived[:rows]) + wide(core_swap(arrived)[rows:])).astype(BF16)

    d_query_far, d_attn, g_r2, g_s2 = pl.pallas_call(
        functools.partial(backward_far_kernel, scale),
        grid=(heads,),
        in_specs=[
            by_head(rows),
            by_head_rows(rows),
            pl.BlockSpec((1, FAR * rows, rows), lambda h: (h, 0, 0)),
            whole(*out_weight.shape),
            by_head(4 * rows),
            by_head(2 * rows, 1),
        ]
        + [whole(rows, cols)] * 5
        + [whole(rows, cols, 1)] * 3
        + [whole(half, cols, 1)],
        out_specs=[by_head_rows(rows), whole(rows, cols), by_head(4 * rows), by_head(2 * rows)],
        out_shape=[
            shape((cols, rows), F32),
            shape((rows, cols), BF16),
            shape((4 * rows, cols), BF16),
            shape((2 * rows, cols), BF16),
        ],
        scratch_shapes=[pltpu.VMEM((rows, cols), BF16)],
        compiler_params=limits,
        cost_estimate=pl.CostEstimate(
            flops=2_500_000_000, bytes_accessed=8_000_000, transcendentals=0
        ),
        name="attend_back_far",
    )(query_act, attn, probs, out_weight, r2, s2, d_both, a1, a2, a3, a4, b1, b2, b3, b4)
    near = PARTS - FAR
    d_query, g_r1, g_s1, g_both = pl.pallas_call(
        functools.partial(backward_near_kernel, scale),
        grid=(heads,),
        in_specs=[
            by_head(rows),
            by_head_rows(rows),
            pl.BlockSpec(
                (pl.Element(1), pl.Element(near * rows), pl.Element(rows)),
                lambda h: (h, FAR * rows, 0),
            ),
            by_head(rows),
            by_head_rows(rows),
        ]
        + [by_head(4 * rows)] * 3,
        out_specs=[by_head(rows)] + [by_head(4 * rows)] * 3,
        out_shape=[shape((rows, cols), BF16)] + [shape((4 * rows, cols), BF16)] * 3,
        compiler_params=limits,
        cost_estimate=pl.CostEstimate(
            flops=4_000_000_000, bytes_accessed=10_000_000, transcendentals=0
        ),
        name="attend_back_near",
    )(query_act, attn, probs, d_attn, d_query_far, r1, s1, both)

    two = 2 * rows
    got = wide(core_swap(g_s2))
    back = jnp.concatenate([g_r2[:two], (wide(g_r2[two:]) + got).astype(BF16)], 0)
    back = chip_step(back, -1)
    back = (wide(g_r1) + wide(core_swap(g_s1)) + wide(back)).astype(BF16)
    back = chip_step(back, -1)
    over = core_swap((wide(g_both[two:]) + wide(back[two:])).astype(BF16))
    total = (wide(g_both[:two]) + wide(back[:two]) + wide(over)).astype(BF16)
    return (output, d_query, total[:rows], total[rows:])


def solution(mesh):
    placed = (
        P("tm", "head"),
        P("tm", "head"),
        P("tm", "head"),
        P("tm", "head"),
        P("head", None),
        P("tm", None),
    )
    return jax.shard_map(
        local,
        mesh=mesh,
        in_specs=placed,
        out_specs=(P("tm", "head"),) * 4,
        check_vma=False,
    )
```

time: 158 us -> 117 us (0.74)
  the two profiles are of different devices: /device:TPU:7 before, /device:TPU:1 now
where the time goes in v1:
time: 117 us
  starting transfers between devices  47.9 us (41%)
  waiting for transfers between devices  40 us (34%)
  Pallas kernels  22.1 us (19%)
  local copies, waits for them, and re-layouts  4.07 us (3%)
  other arithmetic  2.1 us (2%)
    ppermute x8, starting transfers between devices, ring_step(): return lax.ppermute(value, ('tm', 'head'), pairs)  25.3 us
    ppermute x8, waiting for transfers between devices, ring_step(): return lax.ppermute(value, ('tm', 'head'), pairs)  20.7 us
    ppermute x4, waiting for transfers between devices, chip_step(): return lax.ppermute(value, 'tm', pairs)  17.4 us
    ppermute x14, starting transfers between devices, core_swap(): return lax.ppermute(value, 'tm', [(s, s ^ 1) for s in range(count)])  13.8 us
    ppermute x4, starting transfers between devices, chip_step(): return lax.ppermute(value, 'tm', pairs)  8.69 us
    pallas_call x1, Pallas kernels, local(): pl.pallas_call(functools.partial(forward_kernel, scale), grid_spec=pltpu....  8.06 us
    pallas_call x1, Pallas kernels, local(): pl.pallas_call(functools.partial(backward_near_kernel, scale), grid=(head...  6.52 us
    pallas_call x1, Pallas kernels, local(): pl.pallas_call(functools.partial(backward_far_kernel, scale), grid=(heads...  5.09 us
  transfers between devices with their start and end apart: 26, of which 12 were waited for; matrix products, arithmetic and copies ran while one was open for 2% of the time, Pallas kernels for 17%

profile of v1, /device:TPU:1, one launch (start us, length us, event | category | flops | bytes accessed | tf_op | source)
XLA Modules:
  0.0 117.1 jit_solution(1047179629856696466)
XLA Ops:
  0.7 3.3 %collective-permute-start = (bf16[256,384]{1,0:T(8,128)(2,1)}, bf16[256,384]{1,0:T(8,128)(2,1)S(1)}, u32[]{:S(2)}, u32[]{:S(2)}) collective-permute-start(bf16[256,384]{1,0:T(8,128)(2,1)} %own_k.1), channel_id=1, source_target_pairs={{0,8},{8,0},{16,24},{24,16},{32,40},{40,32},{48,56},{56,48},{64,72... | collective-permute-start | bytes 589832 | tf_op jit(solution)/shard_map/ppermute | solution.py:22
  3.9 0.1 collective-permute-start.1
  4.0 0.4 collective-permute-start.2
  4.5 0.8 collective-permute-done.sib_k
  5.2 0.4 collective-permute-done.1.sib_v
  5.6 0.3 collective-permute-done.2.sib_d
  5.9 0.0 copy-done.9
  5.9 0.4 copy-done.10
  6.3 0.7 copy-done.11
  6.9 2.4 %pack.1 = (bf16[1024,384]{1,0:T(8,128)(2,1)}, bf16[512,384]{1,0:T(8,128)(2,1)}) custom-call(bf16[256,384]{1,0:T(8,128)(2,1)} %own_k.1, bf16[256,384]{1,0:T(8,128)(2,1)} %own_v.1, bf16[256,384]{1,0:T(8,128)(2,1)} %own_d.1, bf16[256,384]{1,0:T(8,128)(2,1)} %copy-done.9, bf16[256,384]{1,0:T(8,128)(2,1)} %copy-done.10, bf16[256,384]{1,0:T(8,128)(2,1)} %copy-done.11), custom_call_target="tpu_custom_call" | custom-call | tf_op jit(solution)/shard_map/pack/pallas_call | solution.py:244
  9.4 3.3 %collective-permute-start.3 = (bf16[1024,384]{1,0:T(8,128)(2,1)}, bf16[1024,384]{1,0:T(8,128)(2,1)}, u32[]{:S(2)}, u32[]{:S(2)}) collective-permute-start(bf16[1024,384]{1,0:T(8,128)(2,1)} %get-tuple-element.19.both), channel_id=1, source_target_pairs={{0,16},{8,248},{16,32},{24,8},{32,48},{40,24},{48,64},{56,40},{64,... | collective-permute-start | bytes 2359304 | tf_op jit(solution)/shard_map/ppermute | solution.py:28
  12.7 5.6 %collective-permute-start.13 = (bf16[512,384]{1,0:T(8,128)(2,1)}, bf16[512,384]{1,0:T(8,128)(2,1)S(1)}, u32[]{:S(2)}, u32[]{:S(2)}) collective-permute-start(bf16[512,384]{1,0:T(8,128)(2,1)} %get-tuple-element.25.refs_0_), channel_id=1, source_target_pairs={{0,1},{1,2},{2,3},{3,4},{4,5},{5,6},{6,7},{7,0},{8,15},{9,8},{10,9... | collective-permute-start | bytes 1179656 | tf_op jit(solution)/shard_map/ppermute | solution.py:38
  18.3 3.7 %collective-permute-done.3.r1 = bf16[1024,384]{1,0:T(8,128)(2,1)} collective-permute-done((bf16[1024,384]{1,0:T(8,128)(2,1)}, bf16[1024,384]{1,0:T(8,128)(2,1)}, u32[]{:S(2)}, u32[]{:S(2)}) %collective-permute-start.3) | collective-permute-done | bytes 786464 | tf_op jit(solution)/shard_map/ppermute | solution.py:28
  21.9 5.2 %collective-permute-start.4 = (bf16[1024,384]{1,0:T(8,128)(2,1)}, bf16[1024,384]{1,0:T(8,128)(2,1)S(1)}, u32[]{:S(2)}, u32[]{:S(2)}) collective-permute-start(bf16[1024,384]{1,0:T(8,128)(2,1)} %collective-permute-done.3.r1), channel_id=1, source_target_pairs={{0,16},{8,248},{16,32},{24,8},{32,48},{40,24},{48,64},{56,40},{64,... | collective-permute-start | bytes 2359304 | tf_op jit(solution)/shard_map/ppermute | solution.py:28
  27.2 5.6 %collective-permute-start.14 = (bf16[512,384]{1,0:T(8,128)(2,1)S(1)}, bf16[512,384]{1,0:T(8,128)(2,1)}, u32[]{:S(2)}, u32[]{:S(2)}) collective-permute-start(bf16[512,384]{1,0:T(8,128)(2,1)S(1)} %collective-permute-done.13.refs_1_), channel_id=1, source_target_pairs={{0,1},{1,2},{2,3},{3,4},{4,5},{5,6},{6,7},{7,0},{8,15},{9,8},{10,9... | collective-permute-start | bytes 1179656 | tf_op jit(solution)/shard_map/ppermute | solution.py:38
  32.8 4.7 %collective-permute-done.14.refs_2_ = bf16[512,384]{1,0:T(8,128)(2,1)} collective-permute-done((bf16[512,384]{1,0:T(8,128)(2,1)S(1)}, bf16[512,384]{1,0:T(8,128)(2,1)}, u32[]{:S(2)}, u32[]{:S(2)}) %collective-permute-start.14) | collective-permute-done | bytes 393248 | tf_op jit(solution)/shard_map/ppermute | solution.py:38
  37.5 3.4 %collective-permute-start.15 = (bf16[512,384]{1,0:T(8,128)(2,1)}, bf16[512,384]{1,0:T(8,128)(2,1)S(1)}, u32[]{:S(2)}, u32[]{:S(2)}) collective-permute-start(bf16[512,384]{1,0:T(8,128)(2,1)} %collective-permute-done.14.refs_2_), channel_id=1, source_target_pairs={{0,1},{1,2},{2,3},{3,4},{4,5},{5,6},{6,7},{7,0},{8,15},{9,8},{10,9... | collective-permute-start | bytes 1179656 | tf_op jit(solution)/shard_map/ppermute | solution.py:38
  40.9 0.0 collective-permute-done.4.r2
  40.9 0.5 collective-permute-start.5
  41.4 4.5 %collective-permute-done.15.refs_3_ = bf16[512,384]{1,0:T(8,128)(2,1)S(1)} collective-permute-done((bf16[512,384]{1,0:T(8,128)(2,1)}, bf16[512,384]{1,0:T(8,128)(2,1)S(1)}, u32[]{:S(2)}, u32[]{:S(2)}) %collective-permute-start.15) | collective-permute-done | bytes 393248 | tf_op jit(solution)/shard_map/ppermute | solution.py:38
  46.0 0.1 maximum_select_fusion
  46.0 3.1 %collective-permute-start.16 = (bf16[256,384]{1,0:T(8,128)(2,1)S(1)}, bf16[256,384]{1,0:T(8,128)(2,1)S(1)}, u32[]{:S(2)}, u32[]{:S(2)}) collective-permute-start(bf16[256,384]{1,0:T(8,128)(2,1)S(1)} %maximum_select_fusion), channel_id=1, source_target_pairs={{0,1},{1,2},{2,3},{3,4},{4,5},{5,6},{6,7},{7,0},{8,15},{9,8},{10,9... | collective-permute-start | bytes 589832 | tf_op jit(solution)/shard_map/ppermute | solution.py:38
  49.1 0.5 collective-permute-start.18
  49.6 2.1 %collective-permute-done.16.refs_4_ = bf16[256,384]{1,0:T(8,128)(2,1)S(1)} collective-permute-done((bf16[256,384]{1,0:T(8,128)(2,1)S(1)}, bf16[256,384]{1,0:T(8,128)(2,1)S(1)}, u32[]{:S(2)}, u32[]{:S(2)}) %collective-permute-start.16) | collective-permute-done | bytes 196640 | tf_op jit(solution)/shard_map/ppermute | solution.py:38
  51.7 0.0 collective-permute-start.19
  51.8 0.0 collective-permute-done.6.s1
  51.8 0.5 collective-permute-start.20
  52.3 0.0 collective-permute-done.5.s2
  52.3 0.0 copy-start.4
  52.3 0.9 copy-done.4
  53.2 1.1 copy-done.6
  54.3 8.1 %attend.1 = (bf16[3,2304,256]{2,1,0:T(8,128)(2,1)S(1)}, bf16[384,256]{1,0:T(8,128)(2,1)S(1)}, f32[896,384]{1,0:T(8,128)S(1)}, bf16[896,384]{1,0:T(8,128)(2,1)S(1)}, f32[256,384]{1,0:T(8,128)S(1)}) custom-call(s32[2,64]{1,0:T(2,128)S(1)} %copy-done.8, bf16[256,384]{1,0:T(8,128)(2,1)S(1)} %copy-done.4, bf16[1024,384]{1,0:T(8,128)(2,1)S(1)} %collective-permute-done.4.r2, ...), custom_call_target="tpu_custom_call" | custom-call | flops 4000000000 | bytes 12000000 | tf_op jit(solution)/shard_map/attend/pallas_call | solution.py:271
  62.4 0.1 collective-permute-start.7
  62.5 0.0 collective-permute-done.17.refs_5_
  62.6 0.0 copy-start.5
  62.6 5.1 %attend_back_far.1 = (f32[384,256]{1,0:T(8,128)S(1)}, bf16[256,384]{1,0:T(8,128)(2,1)S(1)}, bf16[1024,384]{1,0:T(8,128)(2,1)S(1)}, bf16[512,384]{1,0:T(8,128)(2,1)S(1)}) custom-call(bf16[256,384]{1,0:T(8,128)(2,1)S(1)} %copy-done.4, bf16[384,256]{1,0:T(8,128)(2,1)S(1)} %get-tuple-element.23.attn, bf16[3,2304,256]{2,1,0:T(8,128)(2,1)S(1)} %get-tuple-element.24.probs, ...), custom_call_target="tpu_custom_call" | custom-call | flops 2500000000 | bytes 8000000 | tf_op jit(solution)/shard_map/attend_back_far/pallas_call | solution.py:328
  67.7 0.6 collective-permute-start.22
  68.3 6.5 %attend_back_near.1 = (bf16[256,384]{1,0:T(8,128)(2,1)}, bf16[1024,384]{1,0:T(8,128)(2,1)S(1)}, bf16[1024,384]{1,0:T(8,128)(2,1)S(1)}, bf16[1024,384]{1,0:T(8,128)(2,1)S(1)}) custom-call(bf16[256,384]{1,0:T(8,128)(2,1)S(1)} %copy-done.5, bf16[384,256]{1,0:T(8,128)(2,1)S(1)} %get-tuple-element.23.attn, bf16[3,2304,256]{2,1,0:T(8,128)(2,1)S(1)} %get-tuple-element.24.probs, ...), custom_call_target="tpu_custom_call" | custom-call | flops 4000000000 | bytes 10000000 | tf_op jit(solution)/shard_map/attend_back_near/pallas_call | solution.py:357
  74.9 0.0 collective-permute-start.21
  74.9 0.1 add_convert_fusion.3
  75.1 3.2 %collective-permute-start.8 = (bf16[256,384]{1,0:T(8,128)(2,1)S(1)}, bf16[256,384]{1,0:T(8,128)(2,1)S(1)}, u32[]{:S(2)}, u32[]{:S(2)}) collective-permute-start(bf16[256,384]{1,0:T(8,128)(2,1)S(1)} %pad_maximum_fusion.4), channel_id=1, source_target_pairs={{0,1},{1,2},{2,3},{3,4},{4,5},{5,6},{6,7},{7,0},{8,15},{9,8},{10,9... | collective-permute-start | bytes 589832 | tf_op jit(solution)/shard_map/ppermute | solution.py:38
  78.2 0.1 pad_maximum_fusion
  78.3 0.1 collective-permute-start.23
  78.4 2.4 %collective-permute-done.8 = bf16[256,384]{1,0:T(8,128)(2,1)S(1)} collective-permute-done((bf16[256,384]{1,0:T(8,128)(2,1)S(1)}, bf16[256,384]{1,0:T(8,128)(2,1)S(1)}, u32[]{:S(2)}, u32[]{:S(2)}) %collective-permute-start.8) | collective-permute-done | bytes 196640 | tf_op jit(solution)/shard_map/ppermute | solution.py:38
  80.9 0.2 add_convert_fusion.6
  81.1 3.2 %collective-permute-start.9 = (bf16[512,384]{1,0:T(8,128)(2,1)S(1)}, bf16[512,384]{1,0:T(8,128)(2,1)S(1)}, u32[]{:S(2)}, u32[]{:S(2)}) collective-permute-start(bf16[512,384]{1,0:T(8,128)(2,1)S(1)} %pad_maximum_fusion.1), channel_id=1, source_target_pairs={{0,1},{1,2},{2,3},{3,4},{4,5},{5,6},{6,7},{7,0},{8,15},{9,8},{10,9... | collective-permute-start | bytes 1179656 | tf_op jit(solution)/shard_map/ppermute | solution.py:38
  84.3 8.2 %collective-permute-done.23 = bf16[1024,384]{1,0:T(8,128)(2,1)S(1)} collective-permute-done((bf16[1024,384]{1,0:T(8,128)(2,1)S(1)}, bf16[1024,384]{1,0:T(8,128)(2,1)S(1)}, u32[]{:S(2)}, u32[]{:S(2)}) %collective-permute-start.23) | collective-permute-done | bytes 786464 | tf_op jit(solution)/shard_map/ppermute | solution.py:28
  92.6 0.3 add_convert_fusion
  92.9 0.1 collective-permute-start.24
  93.0 0.1 convert_element_type.75
  93.0 0.1 fusion.3
  93.2 0.3 collective-permute-start.10
  93.5 6.9 %collective-permute-done.10 = bf16[512,384]{1,0:T(8,128)(2,1)S(1)} collective-permute-done((bf16[512,384]{1,0:T(8,128)(2,1)S(1)}, bf16[512,384]{1,0:T(8,128)(2,1)S(1)}, u32[]{:S(2)}, u32[]{:S(2)}) %collective-permute-start.10) | collective-permute-done | bytes 393248 | tf_op jit(solution)/shard_map/ppermute | solution.py:38
  100.4 0.1 convert_element_type.77
  100.4 0.1 fusion.1
  100.6 1.0 collective-permute-start.11
  101.6 5.5 %collective-permute-done.24 = bf16[1024,384]{1,0:T(8,128)(2,1)S(1)} collective-permute-done((bf16[1024,384]{1,0:T(8,128)(2,1)S(1)}, bf16[1024,384]{1,0:T(8,128)(2,1)S(1)}, u32[]{:S(2)}, u32[]{:S(2)}) %collective-permute-start.24) | collective-permute-done | bytes 786464 | tf_op jit(solution)/shard_map/ppermute | solution.py:28
  107.1 0.1 add_convert_fusion.2
  107.2 0.1 collective-permute-start.25
  107.3 7.7 %collective-permute-start.12 = (bf16[512,384]{1,0:T(8,128)(2,1)S(1)}, bf16[512,384]{1,0:T(8,128)(2,1)S(1)}, u32[]{:S(2)}, u32[]{:S(2)}) collective-permute-start(bf16[512,384]{1,0:T(8,128)(2,1)S(1)} %collective-permute-done.11), channel_id=1, source_target_pairs={{0,8},{8,0},{16,24},{24,16},{32,40},{40,32},{48,56},{56,48},{64,72... | collective-permute-start | bytes 1179656 | tf_op jit(solution)/shard_map/ppermute | solution.py:22
  115.0 0.1 add_convert_fusion.1
  115.2 0.8 fusion.5
  116.0 0.4 collective-permute-done.12
  116.4 0.7 add_convert_fusion.4
  (39 shorter events, 0.3 us)
Async XLA Ops:
  0.6 51.6 %copy-start.8 = (s32[2,64]{1,0:T(2,128)S(1)}, s32[2,64]{1,0:T(2,128)}, u32[]{:S(2)}) copy-start(s32[2,64]{1,0:T(2,128)} %mask.1) | copy-start | bytes 1540
  0.6 51.6 %copy-start = (bf16[384,3072]{1,0:T(8,128)(2,1)S(1)}, bf16[384,3072]{1,0:T(8,128)(2,1)}, u32[]{:S(2)}) copy-start(bf16[384,3072]{1,0:T(8,128)(2,1)} %weight.1) | copy-start | bytes 7077892
  0.7 4.6 %collective-permute-start = (bf16[256,384]{1,0:T(8,128)(2,1)}, bf16[256,384]{1,0:T(8,128)(2,1)S(1)}, u32[]{:S(2)}, u32[]{:S(2)}) collective-permute-start(bf16[256,384]{1,0:T(8,128)(2,1)} %own_k.1), channel_id=1, source_target_pairs={{0,8},{8,0},{16,24},{24,16},{32,40},{40,32},{48,56},{56,48},{64,72... | collective-permute-start | bytes 589832 | tf_op jit(solution)/shard_map/ppermute | solution.py:22
  3.9 1.7 %collective-permute-start.1 = (bf16[256,384]{1,0:T(8,128)(2,1)}, bf16[256,384]{1,0:T(8,128)(2,1)S(1)}, u32[]{:S(2)}, u32[]{:S(2)}) collective-permute-start(bf16[256,384]{1,0:T(8,128)(2,1)} %own_v.1), channel_id=1, source_target_pairs={{0,8},{8,0},{16,24},{24,16},{32,40},{40,32},{48,56},{56,48},{64,72... | collective-permute-start | bytes 589832 | tf_op jit(solution)/shard_map/ppermute | solution.py:22
  4.0 1.8 %collective-permute-start.2 = (bf16[256,384]{1,0:T(8,128)(2,1)}, bf16[256,384]{1,0:T(8,128)(2,1)S(1)}, u32[]{:S(2)}, u32[]{:S(2)}) collective-permute-start(bf16[256,384]{1,0:T(8,128)(2,1)} %own_d.1), channel_id=1, source_target_pairs={{0,8},{8,0},{16,24},{24,16},{32,40},{40,32},{48,56},{56,48},{64,72... | collective-permute-start | bytes 589832 | tf_op jit(solution)/shard_map/ppermute | solution.py:22
  5.2 0.7 copy-start.9
  5.6 0.7 copy-start.10
  6.3 0.7 copy-start.11
  9.4 12.5 %collective-permute-start.3 = (bf16[1024,384]{1,0:T(8,128)(2,1)}, bf16[1024,384]{1,0:T(8,128)(2,1)}, u32[]{:S(2)}, u32[]{:S(2)}) collective-permute-start(bf16[1024,384]{1,0:T(8,128)(2,1)} %get-tuple-element.19.both), channel_id=1, source_target_pairs={{0,16},{8,248},{16,32},{24,8},{32,48},{40,24},{48,64},{56,40},{64,... | collective-permute-start | bytes 2359304 | tf_op jit(solution)/shard_map/ppermute | solution.py:28
  12.7 14.5 %collective-permute-start.13 = (bf16[512,384]{1,0:T(8,128)(2,1)}, bf16[512,384]{1,0:T(8,128)(2,1)S(1)}, u32[]{:S(2)}, u32[]{:S(2)}) collective-permute-start(bf16[512,384]{1,0:T(8,128)(2,1)} %get-tuple-element.25.refs_0_), channel_id=1, source_target_pairs={{0,1},{1,2},{2,3},{3,4},{4,5},{5,6},{6,7},{7,0},{8,15},{9,8},{10,9... | collective-permute-start | bytes 1179656 | tf_op jit(solution)/shard_map/ppermute | solution.py:38
  21.9 18.9 %collective-permute-start.4 = (bf16[1024,384]{1,0:T(8,128)(2,1)}, bf16[1024,384]{1,0:T(8,128)(2,1)S(1)}, u32[]{:S(2)}, u32[]{:S(2)}) collective-permute-start(bf16[1024,384]{1,0:T(8,128)(2,1)} %collective-permute-done.3.r1), channel_id=1, source_target_pairs={{0,16},{8,248},{16,32},{24,8},{32,48},{40,24},{48,64},{56,40},{64,... | collective-permute-start | bytes 2359304 | tf_op jit(solution)/shard_map/ppermute | solution.py:28
  27.2 13.7 %copy-start.2 = (bf16[512,384]{1,0:T(8,128)(2,1)}, bf16[512,384]{1,0:T(8,128)(2,1)S(1)}, u32[]{:S(2)}) copy-start(bf16[512,384]{1,0:T(8,128)(2,1)S(1)} %collective-permute-done.13.refs_1_) | copy-start | bytes 1179652
  27.2 10.3 %collective-permute-start.14 = (bf16[512,384]{1,0:T(8,128)(2,1)S(1)}, bf16[512,384]{1,0:T(8,128)(2,1)}, u32[]{:S(2)}, u32[]{:S(2)}) collective-permute-start(bf16[512,384]{1,0:T(8,128)(2,1)S(1)} %collective-permute-done.13.refs_1_), channel_id=1, source_target_pairs={{0,1},{1,2},{2,3},{3,4},{4,5},{5,6},{6,7},{7,0},{8,15},{9,8},{10,9... | collective-permute-start | bytes 1179656 | tf_op jit(solution)/shard_map/ppermute | solution.py:38
  37.5 8.4 %collective-permute-start.15 = (bf16[512,384]{1,0:T(8,128)(2,1)}, bf16[512,384]{1,0:T(8,128)(2,1)S(1)}, u32[]{:S(2)}, u32[]{:S(2)}) collective-permute-start(bf16[512,384]{1,0:T(8,128)(2,1)} %collective-permute-done.14.refs_2_), channel_id=1, source_target_pairs={{0,1},{1,2},{2,3},{3,4},{4,5},{5,6},{6,7},{7,0},{8,15},{9,8},{10,9... | collective-permute-start | bytes 1179656 | tf_op jit(solution)/shard_map/ppermute | solution.py:38
  40.9 10.9 %collective-permute-start.6 = (bf16[1024,384]{1,0:T(8,128)(2,1)}, bf16[1024,384]{1,0:T(8,128)(2,1)}, u32[]{:S(2)}, u32[]{:S(2)}) collective-permute-start(bf16[1024,384]{1,0:T(8,128)(2,1)} %collective-permute-done.3.r1), channel_id=1, source_target_pairs={{0,8},{8,0},{16,24},{24,16},{32,40},{40,32},{48,56},{56,48},{64,72... | collective-permute-start | bytes 2359304 | tf_op jit(solution)/shard_map/ppermute | solution.py:22
  40.9 11.4 %collective-permute-start.5 = (bf16[1024,384]{1,0:T(8,128)(2,1)S(1)}, bf16[1024,384]{1,0:T(8,128)(2,1)}, u32[]{:S(2)}, u32[]{:S(2)}) collective-permute-start(bf16[1024,384]{1,0:T(8,128)(2,1)S(1)} %collective-permute-done.4.r2), channel_id=1, source_target_pairs={{0,8},{8,0},{16,24},{24,16},{32,40},{40,32},{48,56},{56,48},{64,72... | collective-permute-start | bytes 2359304 | tf_op jit(solution)/shard_map/ppermute | solution.py:22
  46.0 16.5 %copy-start.1 = (bf16[512,384]{1,0:T(8,128)(2,1)S(1)}, bf16[512,384]{1,0:T(8,128)(2,1)}, u32[]{:S(2)}) copy-start(bf16[512,384]{1,0:T(8,128)(2,1)} %get-tuple-element.25.refs_0_) | copy-start | bytes 1179652
  46.0 16.5 %copy-start.3 = (bf16[512,384]{1,0:T(8,128)(2,1)S(1)}, bf16[512,384]{1,0:T(8,128)(2,1)}, u32[]{:S(2)}) copy-start(bf16[512,384]{1,0:T(8,128)(2,1)} %copy-done.2) | copy-start | bytes 1179652
  46.0 5.7 %collective-permute-start.16 = (bf16[256,384]{1,0:T(8,128)(2,1)S(1)}, bf16[256,384]{1,0:T(8,128)(2,1)S(1)}, u32[]{:S(2)}, u32[]{:S(2)}) collective-permute-start(bf16[256,384]{1,0:T(8,128)(2,1)S(1)} %maximum_select_fusion), channel_id=1, source_target_pairs={{0,1},{1,2},{2,3},{3,4},{4,5},{5,6},{6,7},{7,0},{8,15},{9,8},{10,9... | collective-permute-start | bytes 589832 | tf_op jit(solution)/shard_map/ppermute | solution.py:38
  49.1 13.4 %collective-permute-start.17 = (bf16[512,384]{1,0:T(8,128)(2,1)}, bf16[512,384]{1,0:T(8,128)(2,1)S(1)}, u32[]{:S(2)}, u32[]{:S(2)}) collective-permute-start(bf16[512,384]{1,0:T(8,128)(2,1)} %copy-done.2), channel_id=1, source_target_pairs={{0,8},{8,0},{16,24},{24,16},{32,40},{40,32},{48,56},{56,48},{64,72... | collective-permute-start | bytes 1179656 | tf_op jit(solution)/shard_map/ppermute | solution.py:22
  49.1 13.4 %collective-permute-start.18 = (bf16[512,384]{1,0:T(8,128)(2,1)}, bf16[512,384]{1,0:T(8,128)(2,1)S(1)}, u32[]{:S(2)}, u32[]{:S(2)}) collective-permute-start(bf16[512,384]{1,0:T(8,128)(2,1)} %collective-permute-done.14.refs_2_), channel_id=1, source_target_pairs={{0,8},{8,0},{16,24},{24,16},{32,40},{40,32},{48,56},{56,48},{64,72... | collective-permute-start | bytes 1179656 | tf_op jit(solution)/shard_map/ppermute | solution.py:22
  51.7 10.8 %collective-permute-start.19 = (bf16[512,384]{1,0:T(8,128)(2,1)S(1)}, bf16[512,384]{1,0:T(8,128)(2,1)S(1)}, u32[]{:S(2)}, u32[]{:S(2)}) collective-permute-start(bf16[512,384]{1,0:T(8,128)(2,1)S(1)} %collective-permute-done.15.refs_3_), channel_id=1, source_target_pairs={{0,8},{8,0},{16,24},{24,16},{32,40},{40,32},{48,56},{56,48},{64,72... | collective-permute-start | bytes 1179656 | tf_op jit(solution)/shard_map/ppermute | solution.py:22
  51.8 10.8 %collective-permute-start.20 = (bf16[256,384]{1,0:T(8,128)(2,1)S(1)}, bf16[256,384]{1,0:T(8,128)(2,1)S(1)}, u32[]{:S(2)}, u32[]{:S(2)}) collective-permute-start(bf16[256,384]{1,0:T(8,128)(2,1)S(1)} %collective-permute-done.16.refs_4_), channel_id=1, source_target_pairs={{0,8},{8,0},{16,24},{24,16},{32,40},{40,32},{48,56},{56,48},{64,72... | collective-permute-start | bytes 589832 | tf_op jit(solution)/shard_map/ppermute | solution.py:22
  52.3 0.9 copy-start.4
  53.2 1.1 copy-start.6
  62.4 12.6 %collective-permute-start.7 = (bf16[896,384]{1,0:T(8,128)(2,1)S(1)}, bf16[896,384]{1,0:T(8,128)(2,1)S(1)}, u32[]{:S(2)}, u32[]{:S(2)}) collective-permute-start(bf16[896,384]{1,0:T(8,128)(2,1)S(1)} %get-tuple-element.22), channel_id=1, source_target_pairs={{0,8},{8,0},{16,24},{24,16},{32,40},{40,32},{48,56},{56,48},{64,72... | collective-permute-start | bytes 2064392 | tf_op jit(solution)/shard_map/ppermute | solution.py:22
  62.6 5.7 %copy-start.5 = (bf16[256,384]{1,0:T(8,128)(2,1)S(1)}, bf16[256,384]{1,0:T(8,128)(2,1)}, u32[]{:S(2)}) copy-start(bf16[256,384]{1,0:T(8,128)(2,1)} %query.5) | copy-start | bytes 589828
  62.6 5.7 %copy-start.7 = (bf16[1024,384]{1,0:T(8,128)(2,1)S(1)}, bf16[1024,384]{1,0:T(8,128)(2,1)}, u32[]{:S(2)}) copy-start(bf16[1024,384]{1,0:T(8,128)(2,1)} %get-tuple-element.19.both) | copy-start | bytes 2359300
  67.7 7.2 %collective-permute-start.22 = (bf16[512,384]{1,0:T(8,128)(2,1)S(1)}, bf16[512,384]{1,0:T(8,128)(2,1)S(1)}, u32[]{:S(2)}, u32[]{:S(2)}) collective-permute-start(bf16[512,384]{1,0:T(8,128)(2,1)S(1)} %get-tuple-element.33), channel_id=1, source_target_pairs={{0,8},{8,0},{16,24},{24,16},{32,40},{40,32},{48,56},{56,48},{64,72... | collective-permute-start | bytes 1179656 | tf_op jit(solution)/shard_map/ppermute | solution.py:22
  74.9 9.5 %collective-permute-start.21 = (bf16[1024,384]{1,0:T(8,128)(2,1)S(1)}, bf16[1024,384]{1,0:T(8,128)(2,1)S(1)}, u32[]{:S(2)}, u32[]{:S(2)}) collective-permute-start(bf16[1024,384]{1,0:T(8,128)(2,1)S(1)} %get-tuple-element.31), channel_id=1, source_target_pairs={{0,8},{8,0},{16,24},{24,16},{32,40},{40,32},{48,56},{56,48},{64,72... | collective-permute-start | bytes 2359304 | tf_op jit(solution)/shard_map/ppermute | solution.py:22
  75.1 5.8 %collective-permute-start.8 = (bf16[256,384]{1,0:T(8,128)(2,1)S(1)}, bf16[256,384]{1,0:T(8,128)(2,1)S(1)}, u32[]{:S(2)}, u32[]{:S(2)}) collective-permute-start(bf16[256,384]{1,0:T(8,128)(2,1)S(1)} %pad_maximum_fusion.4), channel_id=1, source_target_pairs={{0,1},{1,2},{2,3},{3,4},{4,5},{5,6},{6,7},{7,0},{8,15},{9,8},{10,9... | collective-permute-start | bytes 589832 | tf_op jit(solution)/shard_map/ppermute | solution.py:38
  78.3 14.2 %collective-permute-start.23 = (bf16[1024,384]{1,0:T(8,128)(2,1)S(1)}, bf16[1024,384]{1,0:T(8,128)(2,1)S(1)}, u32[]{:S(2)}, u32[]{:S(2)}) collective-permute-start(bf16[1024,384]{1,0:T(8,128)(2,1)S(1)} %pad_maximum_fusion), channel_id=1, source_target_pairs={{0,240},{8,24},{16,0},{24,40},{32,16},{40,56},{48,32},{56,72},{64,... | collective-permute-start | bytes 2359304 | tf_op jit(solution)/shard_map/ppermute | solution.py:28
  81.1 11.8 %collective-permute-start.9 = (bf16[512,384]{1,0:T(8,128)(2,1)S(1)}, bf16[512,384]{1,0:T(8,128)(2,1)S(1)}, u32[]{:S(2)}, u32[]{:S(2)}) collective-permute-start(bf16[512,384]{1,0:T(8,128)(2,1)S(1)} %pad_maximum_fusion.1), channel_id=1, source_target_pairs={{0,1},{1,2},{2,3},{3,4},{4,5},{5,6},{6,7},{7,0},{8,15},{9,8},{10,9... | collective-permute-start | bytes 1179656 | tf_op jit(solution)/shard_map/ppermute | solution.py:38
  92.9 14.2 %collective-permute-start.24 = (bf16[1024,384]{1,0:T(8,128)(2,1)S(1)}, bf16[1024,384]{1,0:T(8,128)(2,1)S(1)}, u32[]{:S(2)}, u32[]{:S(2)}) collective-permute-start(bf16[1024,384]{1,0:T(8,128)(2,1)S(1)} %add_convert_fusion), channel_id=1, source_target_pairs={{0,240},{8,24},{16,0},{24,40},{32,16},{40,56},{48,32},{56,72},{64,... | collective-permute-start | bytes 2359304 | tf_op jit(solution)/shard_map/ppermute | solution.py:28
  93.2 7.2 %collective-permute-start.10 = (bf16[512,384]{1,0:T(8,128)(2,1)S(1)}, bf16[512,384]{1,0:T(8,128)(2,1)S(1)}, u32[]{:S(2)}, u32[]{:S(2)}) collective-permute-start(bf16[512,384]{1,0:T(8,128)(2,1)S(1)} %pad_maximum_fusion.2), channel_id=1, source_target_pairs={{0,1},{1,2},{2,3},{3,4},{4,5},{5,6},{6,7},{7,0},{8,15},{9,8},{10,9... | collective-permute-start | bytes 1179656 | tf_op jit(solution)/shard_map/ppermute | solution.py:38
  100.6 6.7 %collective-permute-start.11 = (bf16[512,384]{1,0:T(8,128)(2,1)S(1)}, bf16[512,384]{1,0:T(8,128)(2,1)S(1)}, u32[]{:S(2)}, u32[]{:S(2)}) collective-permute-start(bf16[512,384]{1,0:T(8,128)(2,1)S(1)} %pad_maximum_fusion.3), channel_id=1, source_target_pairs={{0,1},{1,2},{2,3},{3,4},{4,5},{5,6},{6,7},{7,0},{8,15},{9,8},{10,9... | collective-permute-start | bytes 1179656 | tf_op jit(solution)/shard_map/ppermute | solution.py:38
  107.2 7.8 %collective-permute-start.25 = (bf16[512,384]{1,0:T(8,128)(2,1)S(1)}, bf16[512,384]{1,0:T(8,128)(2,1)S(1)}, u32[]{:S(2)}, u32[]{:S(2)}) collective-permute-start(bf16[512,384]{1,0:T(8,128)(2,1)S(1)} %add_convert_fusion.2), channel_id=1, source_target_pairs={{0,8},{8,0},{16,24},{24,16},{32,40},{40,32},{48,56},{56,48},{64,72... | collective-permute-start | bytes 1179656 | tf_op jit(solution)/shard_map/ppermute | solution.py:22
  107.3 9.1 %collective-permute-start.12 = (bf16[512,384]{1,0:T(8,128)(2,1)S(1)}, bf16[512,384]{1,0:T(8,128)(2,1)S(1)}, u32[]{:S(2)}, u32[]{:S(2)}) collective-permute-start(bf16[512,384]{1,0:T(8,128)(2,1)S(1)} %collective-permute-done.11), channel_id=1, source_target_pairs={{0,8},{8,0},{16,24},{24,16},{32,40},{40,32},{48,56},{56,48},{64,72... | collective-permute-start | bytes 1179656 | tf_op jit(solution)/shard_map/ppermute | solution.py:22
